TPU v7x, 32 devices: a whole 2x2x4 slice. The times are simulated.
32 devices in a mesh: tgt: 16 (over z, y, core), sup: 2 (over x).
Axes of the slice: x: 2, y: 2, z: 4, core: 2. Of those that a mesh axis runs over, the one named last changes fastest.
Arguments:
- targets: bfloat16 [3584, 12288], P('tgt', 'sup'), may hold values from -6 to 6, as said below
- support: bfloat16 [128, 12288], P('sup'), may hold values from -6 to 6, as said below
- label_weights: bfloat16 [128, 1000], P('sup'), may hold values from -0.00390625 to 0.00390625
- labels: int32 [3584], P('tgt'), may hold values from 0 to 999
- first_moment: float32 [128, 12288], P('sup', 'tgt'), may hold values from -0.6 to 0.6
- second_moment: float32 [128, 12288], P('sup', 'tgt'), may hold values from 0.001 to 0.1
Outputs:
- new_support: bfloat16 [128, 12288], P('sup')
- new_first: float32 [128, 12288], P('sup', 'tgt')
- new_second: float32 [128, 12288], P('sup', 'tgt')
Inputs may be any that keep to these rules, and one draw needn't show every extreme that they name: `targets`: image pixel values. `support`: image pixel values.
All inputs are finite; a program needn't handle non-finite values.
Results may differ from a plain program's by a relative error of at most 0.0028.
Values may be sent and summed in bfloat16 or wider, within the bound.
A program may use at most 64 MiB of HBM per device.

v0:
```python
import math
import jax
import jax.numpy as jnp
from jax import lax
from jax.sharding import PartitionSpec as P

DEPTH = 3
bias_var = 0.1
learning_rate = 0.05
first_decay = 0.9
second_decay = 0.99
first_fix = 1.0 - 0.9**10
second_fix = 1.0 - 0.99**10
adam_eps = 1e-08


def tangent_kernel(cross, target_diag, support_diag):
    tangent = cross
    current = cross
    left_diag = target_diag
    right_diag = support_diag
    for _ in range(DEPTH):
        product = (1.0 + 2.0 * left_diag)[:, None] * (1.0 + 2.0 * right_diag)[None, :]
        slope = 4.0 / math.pi / jnp.sqrt(product - 4.0 * current * current)
        current = 2.0 / math.pi * jnp.arcsin(2.0 * current / jnp.sqrt(product)) + bias_var
        tangent = current + slope * tangent
        left_diag = 2.0 / math.pi * jnp.arcsin(2.0 * left_diag / (1.0 + 2.0 * left_diag)) + bias_var
        right_diag = (
            2.0 / math.pi * jnp.arcsin(2.0 * right_diag / (1.0 + 2.0 * right_diag)) + bias_var
        )
    return tangent


def row_squares(images):
    return jnp.sum(jnp.square(images.astype(jnp.float32)), axis=1)


def shards(targets, support, label_weights, labels, first_moment, second_moment):
    pixels = support.shape[1]
    target_count = targets.shape[0] * lax.axis_size("tgt")
    support_count = support.shape[0] * lax.axis_size("sup")
    class_count = label_weights.shape[1]
    support_diag = row_squares(support) / pixels + bias_var
    slabs = lax.all_to_all(support, "sup", split_axis=1, concat_axis=0, tiled=True)
    partial_cross = lax.dot_general(
        targets, slabs, (((1,), (1,)), ((), ())), preferred_element_type=jnp.float32
    )
    cross = (
        lax.psum_scatter(
            partial_cross.astype(jnp.bfloat16), "sup", scatter_dimension=1, tiled=True
        ).astype(jnp.float32)
        / pixels
        + bias_var
    )
    target_diag = lax.psum(row_squares(targets), "sup") / pixels + bias_var

    def kernel_of(cross_in, diag_in):
        return tangent_kernel(cross_in, target_diag, diag_in)

    kernel, pullback = jax.vjp(kernel_of, cross, support_diag)
    partial_pred = jnp.dot(
        kernel.astype(jnp.bfloat16), label_weights, preferred_element_type=jnp.float32
    )
    predicted = lax.psum(partial_pred.astype(jnp.bfloat16), "sup").astype(jnp.float32)
    classes = jnp.arange(class_count, dtype=jnp.int32)
    onehot = (labels[:, None] == classes[None, :]).astype(jnp.float32)
    residual = (predicted - onehot).astype(jnp.bfloat16)
    kernel_grad = lax.dot_general(
        residual, label_weights, (((1,), (1,)), ((), ())), preferred_element_type=jnp.float32
    )
    kernel_grad = kernel_grad * (
        4.0 * pixels * math.sqrt(class_count * support_count / target_count)
    )
    cross_grad, norm_grad = pullback(kernel_grad)
    cross_low = cross_grad.astype(jnp.bfloat16)
    all_grads = lax.all_gather(cross_low, "sup", axis=1, tiled=True)
    slab_grad = lax.dot_general(
        all_grads, targets, (((0,), (0,)), ((), ())), preferred_element_type=jnp.float32
    )
    image_grad = lax.all_to_all(
        slab_grad.astype(jnp.bfloat16), "sup", split_axis=0, concat_axis=1, tiled=True
    ).astype(slab_grad.dtype)
    gradient = (image_grad + 2.0 * norm_grad[:, None] * support.astype(jnp.float32)) / pixels
    shares = lax.psum_scatter(gradient, "tgt", scatter_dimension=1, tiled=True)
    slab_width = shares.shape[1]
    own_pixels = lax.dynamic_slice_in_dim(
        support, lax.axis_index("tgt") * slab_width, slab_width, 1
    ).astype(jnp.float32)
    new_first = first_decay * first_moment + (1.0 - first_decay) * shares
    new_second = second_decay * second_moment + (1.0 - second_decay) * shares * shares
    update = (
        learning_rate * (new_first / first_fix) / (jnp.sqrt(new_second / second_fix) + adam_eps)
    )
    new_slab = (own_pixels - update).astype(jnp.bfloat16)
    new_support = lax.all_gather(new_slab, "tgt", axis=1, tiled=True)
    return (new_support, new_first, new_second)


def solution(mesh):
    return jax.shard_map(
        shards,
        mesh=mesh,
        in_specs=(
            P("tgt", "sup"),
            P("sup", None),
            P("sup", None),
            P("tgt"),
            P("sup", "tgt"),
            P("sup", "tgt"),
        ),
        out_specs=(P("sup", None), P("sup", "tgt"), P("sup", "tgt")),
        check_vma=False,
    )
```

profile of v0, /device:TPU:0, one launch (start us, length us, event | category | flops | bytes accessed | tf_op | source)
XLA Modules:
  0.0 233.6 jit_solution(4970678291514561601)
XLA Ops:
  7.2 2.8 %copy.18 = bf16[8,2,8,6144]{3,2,0,1:T(8,128)(2,1)} copy(bf16[8,2,8,6144]{3,2,1,0:T(8,128)(2,1)} %bitcast.18) | data formatting | bytes 3145728 | tf_op jit(solution)/shard_map/all_to_all | solution.py:44
  10.0 4.6 %all-to-all-start = ((bf16[64,2,6144]{2,0,1:T(8,128)(2,1)}), bf16[64,2,6144]{2,0,1:T(8,128)(2,1)}, u32[]{:S(2)}, u32[]{:S(2)}) async-start(bf16[64,2,6144]{2,0,1:T(8,128)(2,1)} %bitcast.20), calls=%async_computation | async-start | bytes 3145728 | tf_op jit(solution)/shard_map/all_to_all | solution.py:44
  14.7 0.6 multiply_reduce_fusion
  15.3 20.2 %psum.14 = f32[224]{0:T(256)S(1)} all-reduce(f32[224]{0:T(256)S(1)} %multiply_reduce_fusion), channel_id=1, replica_groups=mesh['tgt'=16,'sup'=2] {'sup'}, use_global_device_ids=true, to_apply=%region_1.0 | all-reduce | flops 224 | bytes 1792 | tf_op jit(solution)/shard_map/psum | solution.py:55
  35.5 1.8 fusion
  37.6 3.1 %convolution_convert_fusion.2 = bf16[224,128]{0,1:T(8,128)(2,1)} fusion(bf16[224,6144]{1,0:T(8,128)(2,1)S(1)} %copy-done.1, bf16[128,6144]{1,0:T(8,128)(2,1)} %bitcast.1), kind=kOutput, calls=%fused_computation.10 | convolution fusion | flops 352350208 | bytes 4382720 | tf_op jit(solution)/shard_map/dot_general | solution.py:45
  40.8 10.6 %reduce-scatter.3.cloned.1.call-done = bf16[224,64]{0,1:T(8,128)(2,1)} async-done(((bf16[224,128]{0,1:T(8,128)(2,1)}), bf16[224,64]{0,1:T(8,128)(2,1)}) %reduce-scatter.3.cloned.1.call-update) | async-done | bytes 28688 | tf_op jit(solution)/shard_map/reduce_scatter | solution.py:49
  51.4 2.6 %convolution_convert_fusion.1 = bf16[224,1000]{1,0:T(8,128)(2,1)} fusion(bf16[64,1000]{1,0:T(8,128)(2,1)S(1)} %copy-done, f32[64]{0:T(128)S(1)} %multiply_add_fusion.7, f32[224]{0:T(256)S(1)} %multiply_add_fusion.6, f32[64]{0:T(128)S(1)} %get-tuple-element.13, f32[224]{0:T(256)S(1)} %get-tuple-element.11, ...), kind=kOutput, calls=%fused_computation.9 | convolution fusion | flops 29641472 | bytes 608128 | tf_op jit(solution)/shard_map/dot_general | solution.py:61
  54.0 27.5 %all-reduce.2.cloned.1.call-done = bf16[224,1000]{1,0:T(8,128)(2,1)} async-done(((bf16[224,1000]{1,0:T(8,128)(2,1)}), bf16[224,1000]{1,0:T(8,128)(2,1)}) %all-reduce.2.cloned.1.call-update) | async-done | bytes 448016 | tf_op jit(solution)/shard_map/psum | solution.py:64
  81.6 1.8 fusion.52
  83.4 0.8 fusion.63
  84.1 0.2 fusion.60
  84.3 4.6 %all_gather.6 = bf16[224,128]{0,1:T(8,128)(2,1)S(1)} all-gather(bf16[224,64]{0,1:T(8,128)(2,1)S(1)} %fusion.60), channel_id=1, replica_groups=mesh['tgt'=16,'sup'=2] {'sup'}, dimensions={1}, use_global_device_ids=true | all-gather | bytes 86016 | tf_op jit(solution)/shard_map/all_gather | solution.py:76
  88.9 1.7 convolution_convert_fusion
  90.6 3.7 %all-to-all-start.1 = ((bf16[2,64,6144]{2,1,0:T(8,128)(2,1)}), bf16[2,64,6144]{2,1,0:T(8,128)(2,1)S(1)}, u32[]{:S(2)}, u32[]{:S(2)}) async-start(bf16[2,64,6144]{2,1,0:T(8,128)(2,1)} %bitcast.21), calls=%async_computation.2 | async-start | bytes 3145728 | tf_op jit(solution)/shard_map/all_to_all | solution.py:80
  94.4 18.1 %all-to-all-done.1 = bf16[2,64,6144]{2,1,0:T(8,128)(2,1)S(1)} async-done(((bf16[2,64,6144]{2,1,0:T(8,128)(2,1)}), bf16[2,64,6144]{2,1,0:T(8,128)(2,1)S(1)}, u32[]{:S(2)}, u32[]{:S(2)}) %all-to-all-start.1) | async-done | bytes 1572896 | tf_op jit(solution)/shard_map/all_to_all | solution.py:80
  112.5 0.3 convert_bitcast_fusion
  112.8 0.2 copy.16
  113.0 1.2 copy-done.2
  114.2 2.2 fusion.2
  116.5 66.4 %reduce-scatter.5.cloned.1.call-done = f32[64,768]{1,0:T(8,128)} async-done(((f32[64,12288]{1,0:T(8,128)}), f32[64,768]{1,0:T(8,128)}) %reduce-scatter.5.cloned.1.call-update) | async-done | bytes 196624 | tf_op jit(solution)/shard_map/reduce_scatter | solution.py:84
  182.9 1.8 subtract_convert_fusion.2
  184.7 39.7 %all-gather.2.cloned.1.call-done = bf16[64,12288]{1,0:T(8,128)(2,1)} async-done(((bf16[64,768]{1,0:T(8,128)(2,1)}), bf16[64,12288]{1,0:T(8,128)(2,1)}) %all-gather.2.cloned.1.call-update) | async-done | bytes 1572880 | tf_op jit(solution)/shard_map/all_gather | solution.py:95
  224.4 2.7 %copy.21 = bf16[64,12288]{1,0:T(8,128)(2,1)} copy(bf16[64,12288]{1,0:T(8,128)(2,1)} %all-gather.2.cloned.1.call-done) | data formatting | bytes 3145728
  (27 shorter events, 0.5 us)
Async XLA Ops:
  7.2 44.3 %copy-start = (bf16[64,1000]{1,0:T(8,128)(2,1)S(1)}, bf16[64,1000]{1,0:T(8,128)(2,1)}, u32[]{:S(2)}) copy-start(bf16[64,1000]{1,0:T(8,128)(2,1)} %param.8) | copy-start | bytes 384004
  7.2 7.5 %copy-start.1 = (bf16[224,6144]{1,0:T(8,128)(2,1)S(1)}, bf16[224,6144]{1,0:T(8,128)(2,1)}, u32[]{:S(2)}) copy-start(bf16[224,6144]{1,0:T(8,128)(2,1)} %param.6) | copy-start | bytes 8257540
  10.0 27.5 %all-to-all-start = ((bf16[64,2,6144]{2,0,1:T(8,128)(2,1)}), bf16[64,2,6144]{2,0,1:T(8,128)(2,1)}, u32[]{:S(2)}, u32[]{:S(2)}) async-start(bf16[64,2,6144]{2,0,1:T(8,128)(2,1)} %bitcast.20), calls=%async_computation | async-start | bytes 3145728 | tf_op jit(solution)/shard_map/all_to_all | solution.py:44
  14.6 36.8 %reduce-scatter.3.cloned.1.call-start = ((), (), s32[]{:S(2)}) async-start(), calls=%async_computation.4 | async-start | bytes 98304 | tf_op jit(solution)/shard_map/reduce_scatter | solution.py:49
  37.5 44.0 %copy-start.6 = (s32[224]{0:T(256)S(1)}, s32[224]{0:T(256)}, u32[]{:S(2)}) copy-start(s32[224]{0:T(256)} %param.9) | copy-start | bytes 2692
  40.7 40.9 %all-reduce.2.cloned.1.call-start = ((), (), s32[]{:S(2)}) async-start(), calls=%async_computation.5 | async-start | bytes 917504 | tf_op jit(solution)/shard_map/psum | solution.py:64
  51.4 30.2 %copy-start.5 = (bf16[224,64]{0,1:T(8,128)(2,1)S(1)}, bf16[224,64]{0,1:T(8,128)(2,1)}, u32[]{:S(2)}) copy-start(bf16[224,64]{0,1:T(8,128)(2,1)} %reduce-scatter.3.cloned.1.call-done) | copy-start | bytes 86020
  90.6 21.8 %all-to-all-start.1 = ((bf16[2,64,6144]{2,1,0:T(8,128)(2,1)}), bf16[2,64,6144]{2,1,0:T(8,128)(2,1)S(1)}, u32[]{:S(2)}, u32[]{:S(2)}) async-start(bf16[2,64,6144]{2,1,0:T(8,128)(2,1)} %bitcast.21), calls=%async_computation.2 | async-start | bytes 3145728 | tf_op jit(solution)/shard_map/all_to_all | solution.py:80
  94.3 88.5 %reduce-scatter.5.cloned.1.call-start = ((), (), s32[]{:S(2)}) async-start(), calls=%async_computation.6 | async-start | bytes 3342336 | tf_op jit(solution)/shard_map/reduce_scatter | solution.py:84
  112.8 1.4 copy-start.2
  116.4 66.5 %copy-start.3 = (f32[64,768]{1,0:T(8,128)S(1)}, f32[64,768]{1,0:T(8,128)}, u32[]{:S(2)}) copy-start(f32[64,768]{1,0:T(8,128)} %param.10) | copy-start | bytes 589828
  116.4 66.5 %copy-start.4 = (f32[64,768]{1,0:T(8,128)S(1)}, f32[64,768]{1,0:T(8,128)}, u32[]{:S(2)}) copy-start(f32[64,768]{1,0:T(8,128)} %param.11) | copy-start | bytes 589828
  116.4 108.0 %all-gather.2.cloned.1.call-start = ((), (), s32[]{:S(2)}) async-start(), calls=%async_computation.7 | async-start | bytes 1671168 | tf_op jit(solution)/shard_map/all_gather | solution.py:95
Sparse Core Ops, SparseCore 0:
  40.8 10.5 reduce-scatter.2
  54.3 27.2 all-reduce.1
  116.5 66.2 reduce-scatter.4
  185.5 38.8 all-gather.1
where the time goes:
time: 234 us
  waiting for transfers between devices  162 us (69%)
  blocking collectives  24.8 us (11%)
  between operations  13.9 us (6%)
  matrix products  9.22 us (4%)
  starting transfers between devices  8.44 us (4%)
  other arithmetic  7.9 us (3%)
  local copies, waits for them, and re-layouts  6.92 us (3%)
    reduce_scatter x1, waiting for transfers between devices, shards(): shares = lax.psum_scatter(gradient, 'tgt', scatter_dimension=1, tiled=True)  66.4 us
    all_gather x1, waiting for transfers between devices, shards(): new_support = lax.all_gather(new_slab, 'tgt', axis=1, tiled=True)  39.7 us
    psum x1, waiting for transfers between devices, shards(): lax.psum(partial_pred.astype(jnp.bfloat16), 'sup').astype(jnp.float32)  27.5 us
    psum x1, blocking collectives, shards(): target_diag = lax.psum(row_squares(targets), 'sup') / pixels + bias_var  20.2 us
    all_to_all x1, waiting for transfers between devices, shards(): lax.all_to_all(slab_grad.astype(jnp.bfloat16), 'sup', split_axis=0, conca...  18.1 us
    reduce_scatter x1, waiting for transfers between devices, shards(): lax.psum_scatter(partial_cross.astype(jnp.bfloat16), 'sup', scatter_dimen...  10.6 us
  transfers between devices with their start and end apart: 6, of which 5 were waited for; matrix products, arithmetic and copies ran while one was open for 1% of the time, Pallas kernels for 0%

commit v1 on v0

--- a/solution.py
+++ b/solution.py
@@ -92,7 +92,24 @@
         learning_rate * (new_first / first_fix) / (jnp.sqrt(new_second / second_fix) + adam_eps)
     )
     new_slab = (own_pixels - update).astype(jnp.bfloat16)
-    new_support = lax.all_gather(new_slab, "tgt", axis=1, tiled=True)
+    size, mine, rows = (lax.axis_size("tgt"), lax.axis_index("tgt"), new_slab.shape[1])
+    right = [(i, (i + 1) % size) for i in range(size)]
+    left = [(i, (i - 1) % size) for i in range(size)]
+    whole = jnp.zeros((*new_slab.shape[:1], size * rows, *new_slab.shape[1 + 1 :]), new_slab.dtype)
+    whole = lax.dynamic_update_slice_in_dim(whole, new_slab, mine * rows, axis=1)
+    from_left = from_right = new_slab
+    half = size // 2
+    for hop in range(1, half + 1):
+        from_left = lax.ppermute(from_left, "tgt", right)
+        whole = lax.dynamic_update_slice_in_dim(
+            whole, from_left, (mine - hop) % size * rows, axis=1
+        )
+        if hop < size - half:
+            from_right = lax.ppermute(from_right, "tgt", left)
+            whole = lax.dynamic_update_slice_in_dim(
+                whole, from_right, (mine + hop) % size * rows, axis=1
+            )
+    new_support = whole
     return (new_support, new_first, new_second)
 
 

time: 234 us -> 248 us (1.060)
  starting transfers between devices: 8.44 us -> 40.5 us
  waiting for transfers between devices: 162 us -> 145 us
    all_gather x1 -> x0, waiting for transfers between devices: 39.7 us -> none  [shards(): new_support = lax.all_gather(new_slab, 'tgt', axis=1, tiled=True)]
    ppermute x0 -> x15, starting transfers between devices: none -> 31.8 us  [the longest x7 31.8 us: shards(): from_right = lax.ppermute(from_right, 'tgt', left)]
    ppermute x0 -> x15, waiting for transfers between devices: none -> 22.3 us  [the longest x8 21.8 us: shards(): from_left = lax.ppermute(from_left, 'tgt', right)]
  transfers between devices with their start and end apart: 6 -> 20, of which waited for: 5 -> 16; matrix products, arithmetic and copies ran while one was open for 1% -> 1% of each run, Pallas kernels for 0% -> 0%
where the time goes in v1:
time: 248 us
  waiting for transfers between devices  145 us (58%)
  starting transfers between devices  40.5 us (16%)
  blocking collectives  24.8 us (10%)
  between operations  14 us (6%)
  matrix products  9.22 us (4%)
  other arithmetic  7.88 us (3%)
  local copies, waits for them, and re-layouts  6.38 us (3%)
    reduce_scatter x1, waiting for transfers between devices, shards(): shares = lax.psum_scatter(gradient, 'tgt', scatter_dimension=1, tiled=True)  66.4 us
    ppermute x7, starting transfers between devices, shards(): from_right = lax.ppermute(from_right, 'tgt', left)  31.8 us
    psum x1, waiting for transfers between devices, shards(): lax.psum(partial_pred.astype(jnp.bfloat16), 'sup').astype(jnp.float32)  27.5 us
    ppermute x8, waiting for transfers between devices, shards(): from_left = lax.ppermute(from_left, 'tgt', right)  21.8 us
    psum x1, blocking collectives, shards(): target_diag = lax.psum(row_squares(targets), 'sup') / pixels + bias_var  20.2 us
    all_to_all x1, waiting for transfers between devices, shards(): lax.all_to_all(slab_grad.astype(jnp.bfloat16), 'sup', split_axis=0, conca...  18.1 us
    reduce_scatter x1, waiting for transfers between devices, shards(): lax.psum_scatter(partial_cross.astype(jnp.bfloat16), 'sup', scatter_dimen...  10.6 us
  transfers between devices with their start and end apart: 20, of which 16 were waited for; matrix products, arithmetic and copies ran while one was open for 1% of the time, Pallas kernels for 0%

profile of v1, /device:TPU:0, one launch (start us, length us, event | category | flops | bytes accessed | tf_op | source)
XLA Modules:
  0.0 247.7 jit_solution(11171423584132606758)
XLA Ops:
  7.2 2.7 %copy.18 = bf16[8,2,8,6144]{3,2,0,1:T(8,128)(2,1)} copy(bf16[8,2,8,6144]{3,2,1,0:T(8,128)(2,1)} %bitcast.18) | data formatting | bytes 3145728 | tf_op jit(solution)/shard_map/all_to_all | solution.py:44
  9.9 4.9 %all-to-all-start = ((bf16[64,2,6144]{2,0,1:T(8,128)(2,1)}), bf16[64,2,6144]{2,0,1:T(8,128)(2,1)}, u32[]{:S(2)}, u32[]{:S(2)}) async-start(bf16[64,2,6144]{2,0,1:T(8,128)(2,1)} %bitcast.20), calls=%async_computation | async-start | bytes 3145728 | tf_op jit(solution)/shard_map/all_to_all | solution.py:44
  15.5 20.2 %psum.14 = f32[224]{0:T(256)S(1)} all-reduce(f32[224]{0:T(256)S(1)} %multiply_reduce_fusion), channel_id=1, replica_groups=mesh['tgt'=16,'sup'=2] {'sup'}, use_global_device_ids=true, to_apply=%region_1.0 | all-reduce | flops 224 | bytes 1792 | tf_op jit(solution)/shard_map/psum | solution.py:55
  37.7 3.1 %convolution_convert_fusion.2 = bf16[224,128]{0,1:T(8,128)(2,1)} fusion(bf16[224,6144]{1,0:T(8,128)(2,1)S(1)} %copy-done.1, bf16[128,6144]{1,0:T(8,128)(2,1)} %bitcast.1), kind=kOutput, calls=%fused_computation.10 | convolution fusion | flops 352350208 | bytes 4382720 | tf_op jit(solution)/shard_map/dot_general | solution.py:45
  41.0 10.6 %reduce-scatter.3.cloned.1.call-done = bf16[224,64]{0,1:T(8,128)(2,1)} async-done(((bf16[224,128]{0,1:T(8,128)(2,1)}), bf16[224,64]{0,1:T(8,128)(2,1)}) %reduce-scatter.3.cloned.1.call-update) | async-done | bytes 28688 | tf_op jit(solution)/shard_map/reduce_scatter | solution.py:49
  51.6 2.6 %convolution_convert_fusion.1 = bf16[224,1000]{1,0:T(8,128)(2,1)} fusion(bf16[64,1000]{1,0:T(8,128)(2,1)S(1)} %copy-done, f32[64]{0:T(128)S(1)} %multiply_add_fusion.7, f32[224]{0:T(256)S(1)} %multiply_add_fusion.6, f32[64]{0:T(128)S(1)} %get-tuple-element.14, f32[224]{0:T(256)S(1)} %get-tuple-element.12, ...), kind=kOutput, calls=%fused_computation.9 | convolution fusion | flops 29641472 | bytes 608128 | tf_op jit(solution)/shard_map/dot_general | solution.py:61
  54.2 27.5 %all-reduce.2.cloned.1.call-done = bf16[224,1000]{1,0:T(8,128)(2,1)} async-done(((bf16[224,1000]{1,0:T(8,128)(2,1)}), bf16[224,1000]{1,0:T(8,128)(2,1)}) %all-reduce.2.cloned.1.call-update) | async-done | bytes 448016 | tf_op jit(solution)/shard_map/psum | solution.py:64
  84.5 4.6 %all_gather.3 = bf16[224,128]{0,1:T(8,128)(2,1)S(1)} all-gather(bf16[224,64]{0,1:T(8,128)(2,1)S(1)} %fusion.60), channel_id=1, replica_groups=mesh['tgt'=16,'sup'=2] {'sup'}, dimensions={1}, use_global_device_ids=true | all-gather | bytes 86016 | tf_op jit(solution)/shard_map/all_gather | solution.py:76
  90.8 3.7 %all-to-all-start.1 = ((bf16[2,64,6144]{2,1,0:T(8,128)(2,1)}), bf16[2,64,6144]{2,1,0:T(8,128)(2,1)S(1)}, u32[]{:S(2)}, u32[]{:S(2)}) async-start(bf16[2,64,6144]{2,1,0:T(8,128)(2,1)} %bitcast.21), calls=%async_computation.2 | async-start | bytes 3145728 | tf_op jit(solution)/shard_map/all_to_all | solution.py:80
  94.6 18.1 %all-to-all-done.1 = bf16[2,64,6144]{2,1,0:T(8,128)(2,1)S(1)} async-done(((bf16[2,64,6144]{2,1,0:T(8,128)(2,1)}), bf16[2,64,6144]{2,1,0:T(8,128)(2,1)S(1)}, u32[]{:S(2)}, u32[]{:S(2)}) %all-to-all-start.1) | async-done | bytes 1572896 | tf_op jit(solution)/shard_map/all_to_all | solution.py:80
  114.4 2.2 fusion.2
  116.6 66.4 %reduce-scatter.5.cloned.1.call-done = f32[64,768]{1,0:T(8,128)} async-done(((f32[64,12288]{1,0:T(8,128)}), f32[64,768]{1,0:T(8,128)}) %reduce-scatter.5.cloned.1.call-update) | async-done | bytes 196624 | tf_op jit(solution)/shard_map/reduce_scatter | solution.py:84
  185.7 4.4 %collective-permute-start.1 = (bf16[64,768]{1,0:T(8,128)(2,1)}, bf16[64,768]{1,0:T(8,128)(2,1)S(1)}, u32[]{:S(2)}, u32[]{:S(2)}) collective-permute-start(bf16[64,768]{1,0:T(8,128)(2,1)} %get-tuple-element.7), channel_id=1, source_target_pairs={{0,30},{2,0},{4,2},{6,4},{8,6},{10,8},{12,10},{14,12},{16,14},{18,... | collective-permute-start | bytes 294920 | tf_op jit(solution)/shard_map/ppermute | solution.py:108
  190.1 2.5 %collective-permute-done = bf16[64,768]{1,0:T(8,128)(2,1)S(1)} collective-permute-done((bf16[64,768]{1,0:T(8,128)(2,1)}, bf16[64,768]{1,0:T(8,128)(2,1)S(1)}, u32[]{:S(2)}, u32[]{:S(2)}) %collective-permute-start) | collective-permute-done | bytes 98336 | tf_op jit(solution)/shard_map/ppermute | solution.py:103
  192.7 4.4 %collective-permute-start.3 = (bf16[64,768]{1,0:T(8,128)(2,1)S(1)}, bf16[64,768]{1,0:T(8,128)(2,1)S(1)}, u32[]{:S(2)}, u32[]{:S(2)}) collective-permute-start(bf16[64,768]{1,0:T(8,128)(2,1)S(1)} %collective-permute-done.1), channel_id=1, source_target_pairs={{0,30},{2,0},{4,2},{6,4},{8,6},{10,8},{12,10},{14,12},{16,14},{18,... | collective-permute-start | bytes 294920 | tf_op jit(solution)/shard_map/ppermute | solution.py:108
  197.1 2.3 collective-permute-done.2
  199.4 4.5 %collective-permute-start.5 = (bf16[64,768]{1,0:T(8,128)(2,1)S(1)}, bf16[64,768]{1,0:T(8,128)(2,1)S(1)}, u32[]{:S(2)}, u32[]{:S(2)}) collective-permute-start(bf16[64,768]{1,0:T(8,128)(2,1)S(1)} %collective-permute-done.3), channel_id=1, source_target_pairs={{0,30},{2,0},{4,2},{6,4},{8,6},{10,8},{12,10},{14,12},{16,14},{18,... | collective-permute-start | bytes 294920 | tf_op jit(solution)/shard_map/ppermute | solution.py:108
  204.0 2.2 collective-permute-done.4
  206.2 4.6 %collective-permute-start.7 = (bf16[64,768]{1,0:T(8,128)(2,1)S(1)}, bf16[64,768]{1,0:T(8,128)(2,1)S(1)}, u32[]{:S(2)}, u32[]{:S(2)}) collective-permute-start(bf16[64,768]{1,0:T(8,128)(2,1)S(1)} %collective-permute-done.5), channel_id=1, source_target_pairs={{0,30},{2,0},{4,2},{6,4},{8,6},{10,8},{12,10},{14,12},{16,14},{18,... | collective-permute-start | bytes 294920 | tf_op jit(solution)/shard_map/ppermute | solution.py:108
  210.8 2.1 collective-permute-done.6
  213.0 4.6 %collective-permute-start.9 = (bf16[64,768]{1,0:T(8,128)(2,1)S(1)}, bf16[64,768]{1,0:T(8,128)(2,1)S(1)}, u32[]{:S(2)}, u32[]{:S(2)}) collective-permute-start(bf16[64,768]{1,0:T(8,128)(2,1)S(1)} %collective-permute-done.7), channel_id=1, source_target_pairs={{0,30},{2,0},{4,2},{6,4},{8,6},{10,8},{12,10},{14,12},{16,14},{18,... | collective-permute-start | bytes 294920 | tf_op jit(solution)/shard_map/ppermute | solution.py:108
  219.8 4.6 %collective-permute-start.11 = (bf16[64,768]{1,0:T(8,128)(2,1)S(1)}, bf16[64,768]{1,0:T(8,128)(2,1)S(1)}, u32[]{:S(2)}, u32[]{:S(2)}) collective-permute-start(bf16[64,768]{1,0:T(8,128)(2,1)S(1)} %collective-permute-done.9), channel_id=1, source_target_pairs={{0,30},{2,0},{4,2},{6,4},{8,6},{10,8},{12,10},{14,12},{16,14},{18,... | collective-permute-start | bytes 294920 | tf_op jit(solution)/shard_map/ppermute | solution.py:108
  226.7 4.6 %collective-permute-start.13 = (bf16[64,768]{1,0:T(8,128)(2,1)S(1)}, bf16[64,768]{1,0:T(8,128)(2,1)S(1)}, u32[]{:S(2)}, u32[]{:S(2)}) collective-permute-start(bf16[64,768]{1,0:T(8,128)(2,1)S(1)} %collective-permute-done.11), channel_id=1, source_target_pairs={{0,30},{2,0},{4,2},{6,4},{8,6},{10,8},{12,10},{14,12},{16,14},{18,... | collective-permute-start | bytes 294920 | tf_op jit(solution)/shard_map/ppermute | solution.py:108
  233.5 6.5 %collective-permute-done.14 = bf16[64,768]{1,0:T(8,128)(2,1)S(1)} collective-permute-done((bf16[64,768]{1,0:T(8,128)(2,1)S(1)}, bf16[64,768]{1,0:T(8,128)(2,1)S(1)}, u32[]{:S(2)}, u32[]{:S(2)}) %collective-permute-start.14) | collective-permute-done | bytes 98336 | tf_op jit(solution)/shard_map/ppermute | solution.py:103
  (71 shorter events, 19.7 us)
Async XLA Ops:
  7.2 44.4 %copy-start = (bf16[64,1000]{1,0:T(8,128)(2,1)S(1)}, bf16[64,1000]{1,0:T(8,128)(2,1)}, u32[]{:S(2)}) copy-start(bf16[64,1000]{1,0:T(8,128)(2,1)} %param.8) | copy-start | bytes 384004
  9.9 27.8 %all-to-all-start = ((bf16[64,2,6144]{2,0,1:T(8,128)(2,1)}), bf16[64,2,6144]{2,0,1:T(8,128)(2,1)}, u32[]{:S(2)}, u32[]{:S(2)}) async-start(bf16[64,2,6144]{2,0,1:T(8,128)(2,1)} %bitcast.20), calls=%async_computation | async-start | bytes 3145728 | tf_op jit(solution)/shard_map/all_to_all | solution.py:44
  14.8 36.8 %reduce-scatter.3.cloned.1.call-start = ((), (), s32[]{:S(2)}) async-start(), calls=%async_computation.4 | async-start | bytes 98304 | tf_op jit(solution)/shard_map/reduce_scatter | solution.py:49
  40.8 40.9 %copy-start.7 = (s32[224]{0:T(256)S(1)}, s32[224]{0:T(256)}, u32[]{:S(2)}) copy-start(s32[224]{0:T(256)} %param.9) | copy-start | bytes 2692
  40.9 40.9 %all-reduce.2.cloned.1.call-start = ((), (), s32[]{:S(2)}) async-start(), calls=%async_computation.5 | async-start | bytes 917504 | tf_op jit(solution)/shard_map/psum | solution.py:64
  51.6 30.2 %copy-start.6 = (bf16[224,64]{0,1:T(8,128)(2,1)S(1)}, bf16[224,64]{0,1:T(8,128)(2,1)}, u32[]{:S(2)}) copy-start(bf16[224,64]{0,1:T(8,128)(2,1)} %reduce-scatter.3.cloned.1.call-done) | copy-start | bytes 86020
  90.8 21.8 %all-to-all-start.1 = ((bf16[2,64,6144]{2,1,0:T(8,128)(2,1)}), bf16[2,64,6144]{2,1,0:T(8,128)(2,1)S(1)}, u32[]{:S(2)}, u32[]{:S(2)}) async-start(bf16[2,64,6144]{2,1,0:T(8,128)(2,1)} %bitcast.21), calls=%async_computation.2 | async-start | bytes 3145728 | tf_op jit(solution)/shard_map/all_to_all | solution.py:80
  94.5 88.5 %reduce-scatter.5.cloned.1.call-start = ((), (), s32[]{:S(2)}) async-start(), calls=%async_computation.6 | async-start | bytes 3342336 | tf_op jit(solution)/shard_map/reduce_scatter | solution.py:84
  116.5 66.6 %copy-start.4 = (f32[64,768]{1,0:T(8,128)S(1)}, f32[64,768]{1,0:T(8,128)}, u32[]{:S(2)}) copy-start(f32[64,768]{1,0:T(8,128)} %param.10) | copy-start | bytes 589828
  185.7 6.9 %collective-permute-start = (bf16[64,768]{1,0:T(8,128)(2,1)}, bf16[64,768]{1,0:T(8,128)(2,1)S(1)}, u32[]{:S(2)}, u32[]{:S(2)}) collective-permute-start(bf16[64,768]{1,0:T(8,128)(2,1)} %get-tuple-element.7), channel_id=1, source_target_pairs={{0,2},{2,4},{4,6},{6,8},{8,10},{10,12},{12,14},{14,16},{16,18},{18... | collective-permute-start | bytes 294920 | tf_op jit(solution)/shard_map/ppermute | solution.py:103
  185.7 7.0 %collective-permute-start.1 = (bf16[64,768]{1,0:T(8,128)(2,1)}, bf16[64,768]{1,0:T(8,128)(2,1)S(1)}, u32[]{:S(2)}, u32[]{:S(2)}) collective-permute-start(bf16[64,768]{1,0:T(8,128)(2,1)} %get-tuple-element.7), channel_id=1, source_target_pairs={{0,30},{2,0},{4,2},{6,4},{8,6},{10,8},{12,10},{14,12},{16,14},{18,... | collective-permute-start | bytes 294920 | tf_op jit(solution)/shard_map/ppermute | solution.py:108
  192.6 6.8 %collective-permute-start.2 = (bf16[64,768]{1,0:T(8,128)(2,1)S(1)}, bf16[64,768]{1,0:T(8,128)(2,1)S(1)}, u32[]{:S(2)}, u32[]{:S(2)}) collective-permute-start(bf16[64,768]{1,0:T(8,128)(2,1)S(1)} %collective-permute-done), channel_id=1, source_target_pairs={{0,2},{2,4},{4,6},{6,8},{8,10},{10,12},{12,14},{14,16},{16,18},{18... | collective-permute-start | bytes 294920 | tf_op jit(solution)/shard_map/ppermute | solution.py:103
  192.7 6.8 %collective-permute-start.3 = (bf16[64,768]{1,0:T(8,128)(2,1)S(1)}, bf16[64,768]{1,0:T(8,128)(2,1)S(1)}, u32[]{:S(2)}, u32[]{:S(2)}) collective-permute-start(bf16[64,768]{1,0:T(8,128)(2,1)S(1)} %collective-permute-done.1), channel_id=1, source_target_pairs={{0,30},{2,0},{4,2},{6,4},{8,6},{10,8},{12,10},{14,12},{16,14},{18,... | collective-permute-start | bytes 294920 | tf_op jit(solution)/shard_map/ppermute | solution.py:108
  199.4 6.7 %collective-permute-start.4 = (bf16[64,768]{1,0:T(8,128)(2,1)S(1)}, bf16[64,768]{1,0:T(8,128)(2,1)S(1)}, u32[]{:S(2)}, u32[]{:S(2)}) collective-permute-start(bf16[64,768]{1,0:T(8,128)(2,1)S(1)} %collective-permute-done.2), channel_id=1, source_target_pairs={{0,2},{2,4},{4,6},{6,8},{8,10},{10,12},{12,14},{14,16},{16,18},{18... | collective-permute-start | bytes 294920 | tf_op jit(solution)/shard_map/ppermute | solution.py:103
  199.4 6.7 %collective-permute-start.5 = (bf16[64,768]{1,0:T(8,128)(2,1)S(1)}, bf16[64,768]{1,0:T(8,128)(2,1)S(1)}, u32[]{:S(2)}, u32[]{:S(2)}) collective-permute-start(bf16[64,768]{1,0:T(8,128)(2,1)S(1)} %collective-permute-done.3), channel_id=1, source_target_pairs={{0,30},{2,0},{4,2},{6,4},{8,6},{10,8},{12,10},{14,12},{16,14},{18,... | collective-permute-start | bytes 294920 | tf_op jit(solution)/shard_map/ppermute | solution.py:108
  206.2 6.7 %collective-permute-start.6 = (bf16[64,768]{1,0:T(8,128)(2,1)S(1)}, bf16[64,768]{1,0:T(8,128)(2,1)S(1)}, u32[]{:S(2)}, u32[]{:S(2)}) collective-permute-start(bf16[64,768]{1,0:T(8,128)(2,1)S(1)} %collective-permute-done.4), channel_id=1, source_target_pairs={{0,2},{2,4},{4,6},{6,8},{8,10},{10,12},{12,14},{14,16},{16,18},{18... | collective-permute-start | bytes 294920 | tf_op jit(solution)/shard_map/ppermute | solution.py:103
  206.2 6.8 %collective-permute-start.7 = (bf16[64,768]{1,0:T(8,128)(2,1)S(1)}, bf16[64,768]{1,0:T(8,128)(2,1)S(1)}, u32[]{:S(2)}, u32[]{:S(2)}) collective-permute-start(bf16[64,768]{1,0:T(8,128)(2,1)S(1)} %collective-permute-done.5), channel_id=1, source_target_pairs={{0,30},{2,0},{4,2},{6,4},{8,6},{10,8},{12,10},{14,12},{16,14},{18,... | collective-permute-start | bytes 294920 | tf_op jit(solution)/shard_map/ppermute | solution.py:108
  212.9 6.8 %collective-permute-start.8 = (bf16[64,768]{1,0:T(8,128)(2,1)S(1)}, bf16[64,768]{1,0:T(8,128)(2,1)S(1)}, u32[]{:S(2)}, u32[]{:S(2)}) collective-permute-start(bf16[64,768]{1,0:T(8,128)(2,1)S(1)} %collective-permute-done.6), channel_id=1, source_target_pairs={{0,2},{2,4},{4,6},{6,8},{8,10},{10,12},{12,14},{14,16},{16,18},{18... | collective-permute-start | bytes 294920 | tf_op jit(solution)/shard_map/ppermute | solution.py:103
  213.0 6.8 %collective-permute-start.9 = (bf16[64,768]{1,0:T(8,128)(2,1)S(1)}, bf16[64,768]{1,0:T(8,128)(2,1)S(1)}, u32[]{:S(2)}, u32[]{:S(2)}) collective-permute-start(bf16[64,768]{1,0:T(8,128)(2,1)S(1)} %collective-permute-done.7), channel_id=1, source_target_pairs={{0,30},{2,0},{4,2},{6,4},{8,6},{10,8},{12,10},{14,12},{16,14},{18,... | collective-permute-start | bytes 294920 | tf_op jit(solution)/shard_map/ppermute | solution.py:108
  219.7 6.8 %collective-permute-start.10 = (bf16[64,768]{1,0:T(8,128)(2,1)S(1)}, bf16[64,768]{1,0:T(8,128)(2,1)S(1)}, u32[]{:S(2)}, u32[]{:S(2)}) collective-permute-start(bf16[64,768]{1,0:T(8,128)(2,1)S(1)} %collective-permute-done.8), channel_id=1, source_target_pairs={{0,2},{2,4},{4,6},{6,8},{8,10},{10,12},{12,14},{14,16},{16,18},{18... | collective-permute-start | bytes 294920 | tf_op jit(solution)/shard_map/ppermute | solution.py:103
  219.8 6.8 %collective-permute-start.11 = (bf16[64,768]{1,0:T(8,128)(2,1)S(1)}, bf16[64,768]{1,0:T(8,128)(2,1)S(1)}, u32[]{:S(2)}, u32[]{:S(2)}) collective-permute-start(bf16[64,768]{1,0:T(8,128)(2,1)S(1)} %collective-permute-done.9), channel_id=1, source_target_pairs={{0,30},{2,0},{4,2},{6,4},{8,6},{10,8},{12,10},{14,12},{16,14},{18,... | collective-permute-start | bytes 294920 | tf_op jit(solution)/shard_map/ppermute | solution.py:108
  226.5 6.7 %collective-permute-start.12 = (bf16[64,768]{1,0:T(8,128)(2,1)S(1)}, bf16[64,768]{1,0:T(8,128)(2,1)S(1)}, u32[]{:S(2)}, u32[]{:S(2)}) collective-permute-start(bf16[64,768]{1,0:T(8,128)(2,1)S(1)} %collective-permute-done.10), channel_id=1, source_target_pairs={{0,2},{2,4},{4,6},{6,8},{8,10},{10,12},{12,14},{14,16},{16,18},{18... | collective-permute-start | bytes 294920 | tf_op jit(solution)/shard_map/ppermute | solution.py:103
  226.7 6.8 %collective-permute-start.13 = (bf16[64,768]{1,0:T(8,128)(2,1)S(1)}, bf16[64,768]{1,0:T(8,128)(2,1)S(1)}, u32[]{:S(2)}, u32[]{:S(2)}) collective-permute-start(bf16[64,768]{1,0:T(8,128)(2,1)S(1)} %collective-permute-done.11), channel_id=1, source_target_pairs={{0,30},{2,0},{4,2},{6,4},{8,6},{10,8},{12,10},{14,12},{16,14},{18,... | collective-permute-start | bytes 294920 | tf_op jit(solution)/shard_map/ppermute | solution.py:108
  233.3 6.7 %collective-permute-start.14 = (bf16[64,768]{1,0:T(8,128)(2,1)S(1)}, bf16[64,768]{1,0:T(8,128)(2,1)S(1)}, u32[]{:S(2)}, u32[]{:S(2)}) collective-permute-start(bf16[64,768]{1,0:T(8,128)(2,1)S(1)} %collective-permute-done.12), channel_id=1, source_target_pairs={{0,2},{2,4},{4,6},{6,8},{8,10},{10,12},{12,14},{14,16},{16,18},{18... | collective-permute-start | bytes 294920 | tf_op jit(solution)/shard_map/ppermute | solution.py:103
  (4 other events, 8.4 us)
Sparse Core Ops, SparseCore 0:
  41.0 10.5 reduce-scatter.2
  54.5 27.2 all-reduce.1
  116.7 66.2 reduce-scatter.4
